TPU v7x, 32 devices: a whole 2x2x4 slice. The times are simulated.
32 devices in a mesh: grp: 2 (over y), smp: 4 (over z), blk: 2 (over x), pen: 2 (over core).
Axes of the slice: x: 2, y: 2, z: 4, core: 2. Of those that a mesh axis runs over, the one named last changes fastest.
Arguments:
- allele_matrix: bfloat16 [2048, 4096], P('smp', ('grp', 'blk')), parts along dimension 1, may hold values from -6 to 6
- orthonormal_frames: bfloat16 [8, 512, 512], P(('grp', 'blk')), parts along dimension 0, may hold values from -0.25 to 0.25
- segment_variances: float32 [8, 512], P(('grp', 'blk')), parts along dimension 0, may hold values from 20.48 to 2048
- lambda_grid: float32 [4], replicated, may hold values from 20.48 to 2048
- trait_levels: bfloat16 [2048, 256], P('smp', ('grp', 'pen')), parts along dimension 1, may hold values from -6 to 6
- partition_labels: int32 [2048], P('smp'), may hold values from 0 to 3
- preceding_fits: bfloat16 [4, 2048, 1536], P(('grp', 'pen'), 'smp', 'blk'), parts along dimension 0, may hold values from -6 to 6
Outputs:
- level0_predictions: bfloat16 [2048, 8, 4, 128], P('smp', ('grp', 'blk'), None, 'pen'), parts along dimension 1
- gram_old: float32 [4, 1536, 1536], P(('grp', 'pen'), 'blk', 'smp'), parts along dimension 0
- gram_cross: float32 [4, 16, 1536], P(('grp', 'pen'), 'blk', 'smp'), parts along dimension 0
- gram_new: float32 [4, 16, 16], P(('grp', 'pen'), 'blk'), parts along dimension 0
- fit_old: float32 [4, 1536], P(('grp', 'pen'), 'smp'), parts along dimension 0
- fit_new: float32 [4, 16], P(('grp', 'pen'), 'blk'), parts along dimension 0
There are 2 independent parts, one for each index of `grp`. A program takes and returns all parts, laid end to end along the dimension named above; an argument that names none is the same for every part. Nothing has to cross between parts.
All inputs are finite; a program needn't handle non-finite values.
Results may differ from a plain program's by a relative error of at most 0.018.
Values may be sent and summed in bfloat16 or wider, within the bound.
A program may use at most 64 MiB of HBM per device.

v0:
```python
import jax
import jax.numpy as jnp
from jax import lax
from jax.sharding import PartitionSpec as P

FOLDS = 4


def segment_fitted_trait(
    projected_traits, pairwise_inner, spectral_line, lambda_grid, partition_mask_real
):
    var_width = projected_traits.shape[1]
    prot_width = pairwise_inner.shape[1] // FOLDS
    lambda_grid_size = lambda_grid.shape[0]
    pairwise_inner = pairwise_inner.reshape(var_width, FOLDS, prot_width)
    remainder = jnp.sum(pairwise_inner, axis=1, keepdims=True) - pairwise_inner
    damping_ratio = 1.0 / (spectral_line[:, None] + lambda_grid[None, :])
    ridge_coefficients = (remainder[:, :, None, :] * damping_ratio[:, None, :, None]).astype(
        jnp.bfloat16
    )
    row_count = projected_traits.shape[0]
    running_total = jnp.zeros((row_count, lambda_grid_size * prot_width), jnp.float32)
    for holdout_index in range(FOLDS):
        lookup_table = ridge_coefficients[:, holdout_index].reshape(
            var_width, lambda_grid_size * prot_width
        )
        running_total = running_total + partition_mask_real[
            :, holdout_index : holdout_index + 1
        ] * jnp.dot(projected_traits, lookup_table, preferred_element_type=jnp.float32)
    return running_total.reshape(row_count, lambda_grid_size, prot_width).astype(jnp.bfloat16)


def sum_block(local_cross):
    return lax.psum(local_cross, "smp")


def per_device(
    allele_matrix,
    orthonormal_frames,
    segment_variances,
    lambda_grid,
    trait_levels,
    partition_labels,
    preceding_fits,
):
    row_count = allele_matrix.shape[0]
    block_count = orthonormal_frames.shape[0]
    var_width = orthonormal_frames.shape[1]
    prot_width = trait_levels.shape[1]
    lambda_grid_size = lambda_grid.shape[0]
    sample_total = float(row_count * lax.axis_size("smp"))
    contract = (((0,), (0,)), ((), ()))
    member = partition_labels[:, None] == jnp.arange(FOLDS, dtype=jnp.int32)[None, :]
    partition_mask_real = member.astype(jnp.float32)
    masked = (member.astype(jnp.bfloat16)[:, :, None] * trait_levels[:, None, :]).reshape(
        row_count, FOLDS * prot_width
    )
    rotated_list = []
    local_list = []
    for entry_offset in range(block_count):
        genotype_cols = allele_matrix[:, entry_offset * var_width : (entry_offset + 1) * var_width]
        projected_traits = jnp.dot(
            genotype_cols, orthonormal_frames[entry_offset], preferred_element_type=jnp.float32
        ).astype(jnp.bfloat16)
        rotated_list.append(projected_traits)
        local_list.append(
            lax.dot_general(projected_traits, masked, contract, preferred_element_type=jnp.float32)
        )
    crossed_list = [sum_block(local_cross) for local_cross in local_list]
    pred_list = [
        segment_fitted_trait(
            rotated_list[entry_offset],
            crossed_list[entry_offset],
            segment_variances[entry_offset],
            lambda_grid,
            partition_mask_real,
        )
        for entry_offset in range(block_count)
    ]
    level0_predictions = jnp.stack(pred_list, axis=1)
    added_columns = level0_predictions[:, :, :, 0].reshape(
        row_count, block_count * lambda_grid_size
    )
    target = trait_levels[:, 0:1]
    old_cols = preceding_fits[0]
    old_width = old_cols.shape[1]
    new_width = added_columns.shape[1]
    joined = jnp.concatenate([old_cols, added_columns], axis=1)
    gathered = lax.all_gather(joined, "blk", axis=1, tiled=True)
    shard_count = gathered.shape[1] // joined.shape[1]
    pieces = gathered.reshape(row_count, shard_count, joined.shape[1])
    old_all = pieces[:, :, :old_width].reshape(row_count, shard_count * old_width)
    new_all = pieces[:, :, old_width:].reshape(row_count, shard_count * new_width)
    stacked = jnp.concatenate([old_cols, added_columns, target], axis=1)
    reduced = lax.psum_scatter(
        lax.dot_general(stacked, old_all, contract, preferred_element_type=jnp.float32),
        "smp",
        scatter_dimension=1,
        tiled=True,
    )
    gram_old = reduced[:old_width]
    gram_cross = reduced[old_width : old_width + new_width]
    fit_old = reduced[old_width + new_width :]
    right_side = jnp.concatenate([new_all, target], axis=1)
    small_gram = lax.psum(
        lax.dot_general(added_columns, right_side, contract, preferred_element_type=jnp.float32),
        "smp",
    )
    gram_new = small_gram[:, :-1]
    fit_new = small_gram[:, -1]
    return (
        level0_predictions,
        (gram_old / sample_total)[None],
        (gram_cross / sample_total)[None],
        (gram_new / sample_total)[None],
        fit_old / sample_total,
        (fit_new / sample_total)[None],
    )


def solution(mesh):
    placed = (
        P("smp", ("grp", "blk")),
        P(("grp", "blk"), None, None),
        P(("grp", "blk"), None),
        P(),
        P("smp", ("grp", "pen")),
        P("smp"),
        P(("grp", "pen"), "smp", "blk"),
    )
    return jax.shard_map(
        per_device,
        mesh=mesh,
        in_specs=placed,
        out_specs=(
            P("smp", ("grp", "blk"), None, "pen"),
            P(("grp", "pen"), "blk", "smp"),
            P(("grp", "pen"), "blk", "smp"),
            P(("grp", "pen"), "blk", None),
            P(("grp", "pen"), "smp"),
            P(("grp", "pen"), "blk"),
        ),
        check_vma=False,
    )
```

profile of v0, /device:TPU:0, one launch (start us, length us, event | category | flops | bytes accessed | tf_op | source)
XLA Modules:
  0.0 205.0 jit_solution(1998468806075060013)
XLA Ops:
  7.2 0.0 copy-start.4
  7.2 0.0 copy-start.2
  7.2 0.0 all-reduce.3.cloned.1.call-start
  7.2 0.0 copy-start.6
  7.2 1.7 convolution_convert_fusion
  9.0 1.5 convolution_convert_fusion.1
  10.5 0.0 copy-start.1
  10.5 1.1 fusion.36
  11.6 1.1 fusion.37
  12.7 0.0 all-reduce.3.cloned.1.call-update
  12.8 0.0 all-gather.2.cloned.1.call-start
  12.8 0.0 copy-done.1
  12.8 0.3 copy.19
  13.1 0.3 copy-done.3
  13.4 0.0 copy-done.5
  13.4 0.1 add_divide_fusion.1
  13.5 54.1 %all-reduce.3.cloned.1.call-done = (f32[512,4,64]{0,2,1:T(8,128)}, f32[512,4,64]{0,2,1:T(8,128)}) async-done(((f32[512,4,64]{0,2,1:T(8,128)}, f32[512,4,64]{0,2,1:T(8,128)}), (f32[512,4,64]{0,2,1:T(8,128)}, f32[512,4,64]{0,2,1:T(8,128)})) %all-reduce.3.cloned.1.call-update) | async-done | bytes 1048592 | tf_op jit(solution)/shard_map/psum | solution.py:34
  67.6 1.1 reduce_sum.19
  68.7 1.1 broadcast_subtract_fusion
  70.0 0.5 multiply_convert_fusion
  70.5 0.1 fusion.33
  70.6 0.1 fusion.32
  70.7 0.3 convolution_multiply_fusion.3
  71.0 0.3 convolution_multiply_fusion.7
  71.3 0.3 fusion.2
  71.7 0.3 fusion.5
  72.0 0.3 fusion.1
  72.4 0.3 fusion.4
  72.7 0.3 fusion.7
  73.1 0.3 fusion.6
  73.4 0.1 fusion.26
  73.5 0.9 pad_maximum_fusion
  74.4 0.0 all-gather.2.cloned.1.call-update
  74.4 0.0 reduce-scatter.2.cloned.1.call-start
  74.5 26.7 %all-gather.2.cloned.1.call-done = bf16[512,1552]{0,1:T(8,128)(2,1)} async-done(((bf16[512,776]{0,1:T(8,128)(2,1)}), bf16[512,1552]{0,1:T(8,128)(2,1)}) %all-gather.2.cloned.1.call-update) | async-done | bytes 1589264 | tf_op jit(solution)/shard_map/all_gather | solution.py:89
  101.2 1.5 slice.126
  102.7 3.6 %fusion.9 = f32[777,1536]{1,0:T(8,128)} fusion(bf16[512,1536]{0,1:T(8,128)(2,1)S(1)} %bitcast.73, bf16[512,1]{0,1:T(2,128)(2,1)S(1)} %slice.104, bf16[512,8]{0,1:T(8,128)(2,1)S(1)} %reshape_squeeze.35, bf16[512,768]{0,1:T(8,128)(2,1)S(1)} %bitcast.62), kind=kOutput, calls=%fused_computation.22 | convolution fusion | flops 1224502272 | bytes 7142400 | tf_op jit(solution)/shard_map/dot_general | solution.py:96
  106.3 0.0 reduce-scatter.2.cloned.1.call-update
  106.3 0.8 pad_maximum_fusion.1
  107.2 0.7 slice_bitcast_fusion
  107.9 0.1 fusion.21
  108.0 12.1 %psum.23 = f32[8,17]{1,0:T(8,128)S(1)} all-reduce(f32[8,17]{1,0:T(8,128)S(1)} %fusion.21), channel_id=1, replica_groups=mesh['grp'=2,'smp'=4,'blk'=2,'pen'=2] {'smp'}, use_global_device_ids=true, to_apply=%region_5.0 | all-reduce | flops 136 | bytes 1088 | tf_op jit(solution)/shard_map/psum | solution.py:105
  120.1 0.7 multiply_reduce_fusion
  120.8 0.6 multiply_bitcast_fusion
  121.4 72.1 %reduce-scatter.2.cloned.1.call-done = f32[777,384]{1,0:T(8,128)} async-done(((f32[777,1536]{1,0:T(8,128)}), f32[777,384]{1,0:T(8,128)}) %reduce-scatter.2.cloned.1.call-update) | async-done | bytes 1193488 | tf_op jit(solution)/shard_map/reduce_scatter | solution.py:95
  193.5 1.3 slice_multiply_fusion.2
  194.8 1.3 fusion.27
  196.1 2.4 %fusion.8 = f32[1,768,384]{2,1,0:T(8,128)} fusion(f32[777,384]{1,0:T(8,128)} %reduce-scatter.2.cloned.1.call-done), kind=kLoop, calls=%fused_computation.21 | loop fusion | flops 294912 | bytes 2359296 | tf_op jit(solution)/shard_map/broadcast_in_dim | solution.py:113
  (15 shorter events, 0.2 us)
Async XLA Ops:
  7.2 3.3 %copy-start.4 = (s32[512]{0:T(512)S(1)}, s32[512]{0:T(512)}, u32[]{:S(2)}) copy-start(s32[512]{0:T(512)} %param.12) | copy-start | bytes 6148
  7.2 3.3 %copy-start.2 = (bf16[512,64]{0,1:T(8,128)(2,1)S(1)}, bf16[512,64]{0,1:T(8,128)(2,1)}, u32[]{:S(2)}) copy-start(bf16[512,64]{0,1:T(8,128)(2,1)} %param.11) | copy-start | bytes 196612
  7.2 60.4 %all-reduce.3.cloned.1.call-start = ((), (), s32[]{:S(2)}) async-start(), calls=%async_computation.3 | async-start | bytes 2097152 | tf_op jit(solution)/shard_map/psum | solution.py:34
  7.2 1.7 copy-start.6
  10.5 2.3 %copy-start.1 = (bf16[1,512,768]{2,1,0:T(8,128)(2,1)S(1)}, bf16[1,512,768]{2,1,0:T(8,128)(2,1)}, u32[]{:S(2)}) copy-start(bf16[1,512,768]{2,1,0:T(8,128)(2,1)} %param.13) | copy-start | bytes 2359300
  12.7 0.7 copy-start.3
  12.7 0.7 copy-start.5
  12.8 88.4 %all-gather.2.cloned.1.call-start = ((), (), s32[]{:S(2)}) async-start(), calls=%async_computation.1 | async-start | bytes 2383872 | tf_op jit(solution)/shard_map/all_gather | solution.py:89
  67.6 2.3 %copy-start = (f32[512,4,64]{0,2,1:T(8,128)S(1)}, f32[512,4,64]{0,2,1:T(8,128)}, u32[]{:S(2)}) copy-start(f32[512,4,64]{0,2,1:T(8,128)} %get-tuple-element.7) | copy-start | bytes 1572868
  74.4 119.1 %reduce-scatter.2.cloned.1.call-start = ((), (), s32[]{:S(2)}) async-start(), calls=%async_computation.2 | async-start | bytes 6021120 | tf_op jit(solution)/shard_map/reduce_scatter | solution.py:95
Sparse Core Ops, SparseCore 0:
  12.9 54.6 all-reduce.2
  74.5 26.5 all-gather.1
  106.4 87.0 reduce-scatter.1
where the time goes:
time: 205 us
  waiting for transfers between devices  153 us (75%)
  between operations  14 us (7%)
  blocking collectives  12.1 us (6%)
  matrix products  11.8 us (6%)
  other arithmetic  11 us (5%)
  local copies, waits for them, and re-layouts  3.02 us (1%)
    reduce_scatter x1, waiting for transfers between devices, per_device(): lax.psum_scatter(lax.dot_general(stacked, old_all, contract, preferred_el...  72.1 us
    psum x1, waiting for transfers between devices, sum_block(): return lax.psum(local_cross, 'smp')  54.1 us
    all_gather x1, waiting for transfers between devices, per_device(): gathered = lax.all_gather(joined, 'blk', axis=1, tiled=True)  26.7 us
    psum x1, blocking collectives, per_device(): lax.psum(lax.dot_general(added_columns, right_side, contract, preferred_e...  12.1 us
  transfers between devices with their start and end apart: 3, of which 3 were waited for; matrix products, arithmetic and copies ran while one was open for 2% of the time, Pallas kernels for 0%

commit v1 on v0

--- a/solution.py
+++ b/solution.py
@@ -1,9 +1,388 @@
+import functools
+import math
+
 import jax
 import jax.numpy as jnp
 from jax import lax
+from jax.experimental import pallas as pl
+from jax.experimental.pallas import tpu as pltpu
 from jax.sharding import PartitionSpec as P
 
 FOLDS = 4
+F32 = jnp.float32
+BF16 = jnp.bfloat16
+MESH = pl.DeviceIdType.MESH
+
+
+def row_piece(total):
+    return next(size for size in (256, 128) if total % size == 0)
+
+
+def kernel(
+    n, nb, groups,
+    allele, frames, variances, lam, trait, labels, old,
+    preds_out, gram_out, cross_out, new_out, fit_old_out, fit_new_out,
+    oldq, old_t, rot, part, c_left, c_right, c_send,
+    g_left, g_right, g_send, g_part, et_all, lhs, m_send, m_recv, m_sum,
+    x_send, x_recv, cs_send, cs_recv, gs_send, gl_recv, gr_recv,
+    e_send, e_recv, ms_send, ms_recv,
+):
+    z = lax.axis_index("smp")
+    x = lax.axis_index("blk")
+    rows, old_width = old.shape
+    blocks, width = frames.shape[0], frames.shape[1]
+    prot = trait.shape[1]
+    lams = groups
+    per = n // nb
+    qw = old_width // per
+    cp = row_piece(blocks * width)
+    c_pieces = blocks * width // cp
+    gp = row_piece(old_width)
+    g_pieces = old_width // gp
+    new_width = blocks * lams
+    erows = et_all.shape[1]
+    sample_total = float(rows * n)
+    order = []
+    for i in range(n // 2):
+        order += [n - 1 - i, i]
+
+    barrier = pltpu.get_barrier_semaphore()
+    for d in range(1, n):
+        pl.semaphore_signal(barrier, inc=1, device_id={"smp": lax.rem(z + d, n)}, device_id_type=MESH)
+    for d in range(1, nb):
+        pl.semaphore_signal(barrier, inc=1, device_id={"blk": lax.rem(x + d, nb)}, device_id_type=MESH)
+    pl.semaphore_wait(barrier, n - 1 + nb - 1)
+
+    def x_copy(q, d):
+        cols = pl.ds(pl.multiple_of((q - x * per) * qw, qw), qw)
+        return pltpu.make_async_remote_copy(
+            src_ref=old.at[:, cols], dst_ref=oldq.at[q], send_sem=x_send.at[q, d], recv_sem=x_recv.at[q],
+            device_id={"blk": lax.rem(x + d, nb)}, device_id_type=MESH)
+
+    def x_wait(q):
+        pltpu.make_async_remote_copy(
+            src_ref=oldq.at[q], dst_ref=oldq.at[q], send_sem=x_send.at[q, 0], recv_sem=x_recv.at[q],
+            device_id={"blk": lax.rem(x + 1, nb)}, device_id_type=MESH).wait_recv()
+
+    for q in order:
+        @pl.when(x == q // per)
+        def _():
+            for d in range(1, nb):
+                x_copy(q, d).start()
+
+    label = labels[...]
+    y = trait[...]
+    y_wide = jnp.concatenate([y] * FOLDS, axis=1)
+    fold_of = lax.broadcasted_iota(jnp.int32, (rows, FOLDS * prot), 1) // prot
+    masked = jnp.where(label == fold_of, y_wide.astype(F32), 0.0).astype(BF16)
+
+    def c_copy(p, right):
+        piece = pl.ds(p * cp, cp)
+        return pltpu.make_async_remote_copy(
+            src_ref=c_send.at[0 if right else 1, piece, :],
+            dst_ref=(c_left if right else c_right).at[piece, :],
+            send_sem=cs_send.at[0 if right else 1, p], recv_sem=cs_recv.at[0 if right else 1, p],
+            device_id={"smp": jnp.minimum(z + 1, n - 1) if right else jnp.maximum(z - 1, 0)}, device_id_type=MESH)
+
+    for b in range(blocks):
+        r = jnp.dot(allele[:, b * width:(b + 1) * width], frames[b], preferred_element_type=F32).astype(BF16)
+        rot[b] = r
+        part[b * width:(b + 1) * width, :] = lax.dot_general(
+            r, masked, (((0,), (0,)), ((), ())), preferred_element_type=F32)
+        for p in range(b * width // cp, (b + 1) * width // cp):
+            value = part[p * cp:(p + 1) * cp, :].astype(BF16)
+
+            @pl.when(z == 0)
+            def _():
+                c_send[0, p * cp:(p + 1) * cp, :] = value
+                c_copy(p, True).start()
+
+            @pl.when(z == n - 1)
+            def _():
+                c_send[1, p * cp:(p + 1) * cp, :] = value
+                c_copy(p, False).start()
+
+    for h in range(per):
+        oldq[x * per + h] = old[:, h * qw:(h + 1) * qw]
+    old_t[...] = old[...].T
+    for q in order:
+        @pl.when(x != q // per)
+        def _():
+            x_wait(q)
+
+    def g_copy(q, h, right):
+        piece = pl.ds(pl.multiple_of(h * gp, gp), gp)
+        return pltpu.make_async_remote_copy(
+            src_ref=g_send.at[q, piece, :],
+            dst_ref=(g_left if right else g_right).at[q, piece, :],
+            send_sem=gs_send.at[q, h], recv_sem=(gl_recv if right else gr_recv).at[q, h],
+            device_id={"smp": jnp.minimum(z + 1, n - 1) if right else jnp.maximum(z - 1, 0)}, device_id_type=MESH)
+
+    def g_piece(q, h):
+        piece = pl.ds(pl.multiple_of(h * gp, gp), gp)
+        g_part[...] = jnp.dot(old_t[piece, :], oldq[q], preferred_element_type=F32)
+
+        @pl.when(z < q)
+        def _():
+            @pl.when(z > 0)
+            def _():
+                g_copy(q, h, True).wait_recv()
+                g_part[...] += g_left[q, piece, :].astype(F32)
+            g_send[q, piece, :] = g_part[...].astype(BF16)
+            g_copy(q, h, True).start()
+
+        @pl.when(z > q)
+        def _():
+            @pl.when(z < n - 1)
+            def _():
+                g_copy(q, h, False).wait_recv()
+                g_part[...] += g_right[q, piece, :].astype(F32)
+            g_send[q, piece, :] = g_part[...].astype(BF16)
+            g_copy(q, h, False).start()
+
+        @pl.when(z == q)
+        def _():
+            @pl.when(z > 0)
+            def _():
+                g_copy(q, h, True).wait_recv()
+                g_part[...] += g_left[q, piece, :].astype(F32)
+
+            @pl.when(z < n - 1)
+            def _():
+                g_copy(q, h, False).wait_recv()
+                g_part[...] += g_right[q, piece, :].astype(F32)
+            gram_out[piece, :] = g_part[...] / sample_total
+
+    def g_group(q):
+        def body(h, carry):
+            g_piece(q, h)
+            return carry
+        lax.fori_loop(0, g_pieces, body, 0)
+
+    in_left = z < n // 2
+    is_end = jnp.logical_or(z == 0, z == n - 1)
+
+    @pl.when(is_end)
+    def _():
+        g_group(jnp.where(in_left, n - 1, 0))
+
+    def from_side(p, right):
+        piece = slice(p * cp, (p + 1) * cp)
+        has = z > 0 if right else z < n - 1
+        forward = z < n - 1 if right else z > 0
+
+        @pl.when(has)
+        def _():
+            c_copy(p, right).wait_recv()
+
+            @pl.when(forward)
+            def _():
+                got = (c_left if right else c_right)[piece, :]
+                c_send[0 if right else 1, piece, :] = (part[piece, :] + got.astype(F32)).astype(BF16)
+                c_copy(p, right).start()
+
+    for first in (True, False):
+        for p in range(c_pieces):
+            @pl.when(in_left)
+            def _():
+                from_side(p, first)
+
+            @pl.when(jnp.logical_not(in_left))
+            def _():
+                from_side(p, not first)
+
+    @pl.when(z > 0)
+    def _():
+        part[...] += c_left[...].astype(F32)
+
+    @pl.when(z < n - 1)
+    def _():
+        part[...] += c_right[...].astype(F32)
+
+    lam_lane = lax.broadcasted_iota(jnp.int32, (1, lams * prot), 1) // prot
+    lam_wide = jnp.zeros((1, lams * prot), F32)
+    for r in range(lams):
+        lam_wide = jnp.where(lam_lane == r, lam[r], lam_wide)
+    sel_rows = lax.broadcasted_iota(jnp.int32, (erows, lams * prot), 0)
+    sel_cols = lax.broadcasted_iota(jnp.int32, (erows, lams * prot), 1)
+    e0 = jnp.zeros((erows, rows), F32)
+    for b in range(blocks):
+        damp = 1.0 / (variances[:, b:b + 1] + lam_wide)
+        c = part[b * width:(b + 1) * width, :]
+        folds = [c[:, k * prot:(k + 1) * prot] for k in range(FOLDS)]
+        total = folds[0]
+        for k in range(1, FOLDS):
+            total = total + folds[k]
+        acc = jnp.zeros((rows, lams * prot), F32)
+        for k in range(FOLDS):
+            rest = jnp.concatenate([total - folds[k]] * lams, axis=1)
+            coeff = (rest * damp).astype(BF16)
+            acc = jnp.where(label == k, jnp.dot(rot[b], coeff, preferred_element_type=F32), acc)
+        pred = acc.astype(BF16)
+        preds_out[:, b * lams * prot:(b + 1) * lams * prot] = pred
+        wanted = x * new_width + b * lams + sel_cols // prot
+        sel = jnp.where(jnp.logical_and(sel_rows == wanted, sel_cols % prot == 0), 1.0, 0.0).astype(BF16)
+        e0 = e0 + lax.dot_general(sel, pred, (((1,), (1,)), ((), ())), preferred_element_type=F32)
+    et_all[x] = e0.astype(BF16)
+
+    def e_copy(d):
+        return pltpu.make_async_remote_copy(
+            src_ref=et_all.at[x], dst_ref=et_all.at[x], send_sem=e_send.at[d], recv_sem=e_recv.at[d],
+            device_id={"blk": lax.rem(x + d, nb)}, device_id_type=MESH)
+
+    def e_wait(d):
+        slot = lax.rem(x + nb - d, nb)
+        pltpu.make_async_remote_copy(
+            src_ref=et_all.at[slot], dst_ref=et_all.at[slot], send_sem=e_send.at[d], recv_sem=e_recv.at[d],
+            device_id={"blk": slot}, device_id_type=MESH).wait_recv()
+
+    for d in range(1, nb):
+        e_copy(d).start()
+    t_rows = lax.broadcasted_iota(jnp.int32, (erows, prot), 0)
+    t_cols = lax.broadcasted_iota(jnp.int32, (erows, prot), 1)
+    t_sel = jnp.where(jnp.logical_and(t_rows == nb * new_width, t_cols == 0), 1.0, 0.0).astype(BF16)
+    target = lax.dot_general(t_sel, y, (((1,), (1,)), ((), ())), preferred_element_type=F32)
+    lhs[...] = (e0 + target).astype(BF16)
+    for q in range(n):
+        m_send[q, :, :qw] = jnp.dot(lhs[...], oldq[q], preferred_element_type=F32)
+    for d in range(1, nb):
+        e_wait(d)
+    right_side = target
+    for b in range(nb):
+        right_side = right_side + et_all[b].astype(F32)
+    small = lax.dot_general(
+        lhs[...], jnp.concatenate([right_side.astype(BF16), jnp.zeros((128 - erows, rows), BF16)], axis=0),
+        (((1,), (1,)), ((), ())), preferred_element_type=F32)
+    for q in range(n):
+        m_send[q, :, qw:] = small
+
+    def m_copy(d):
+        return pltpu.make_async_remote_copy(
+            src_ref=m_send.at[lax.rem(z + d, n)], dst_ref=m_recv.at[d], send_sem=ms_send.at[d], recv_sem=ms_recv.at[d],
+            device_id={"smp": lax.rem(z + d, n)}, device_id_type=MESH)
+
+    for d in range(1, n):
+        m_copy(d).start()
+
+    for i in range(n // 2):
+        early = jnp.where(in_left, n - 1 - i, i)
+        late = n - 1 - early
+        if i == 0:
+            @pl.when(jnp.logical_not(is_end))
+            def _():
+                g_group(early)
+        else:
+            @pl.when(early != z)
+            def _():
+                g_group(early)
+
+        @pl.when(late != z)
+        def _():
+            g_group(late)
+    g_group(z)
+
+    total = m_send[z]
+    for d in range(1, n):
+        m_copy(d).wait_recv()
+        total = total + m_recv[d]
+    m_sum[...] = total / sample_total
+    mine = pl.ds(pl.multiple_of(x * new_width, 8), new_width)
+    cross_out[...] = m_sum[mine, :qw]
+    tail = m_sum[mine, qw:]
+    new_out[...] = tail[:, :nb * new_width]
+    lane = lax.broadcasted_iota(jnp.int32, tail.shape, 1)
+    fit_new_out[...] = jnp.sum(jnp.where(lane == nb * new_width, tail, 0.0), axis=1, keepdims=True)
+    fit_old_out[...] = m_sum[nb * new_width:nb * new_width + 1, :qw]
+
+    for q in range(n):
+        @pl.when(x == q // per)
+        def _():
+            for d in range(1, nb):
+                x_copy(q, d).wait_send()
+    for p in range(c_pieces):
+        @pl.when(z < n - 1)
+        def _():
+            c_copy(p, True).wait_send()
+
+        @pl.when(z > 0)
+        def _():
+            c_copy(p, False).wait_send()
+    for d in range(1, nb):
+        e_copy(d).wait_send()
+    for d in range(1, n):
+        m_copy(d).wait_send()
+    for q in range(n):
+        @pl.when(z != q)
+        def _():
+            for h in range(g_pieces):
+                g_copy(q, h, True).wait_send()
+
+
+def fused(
+    n, nb, allele_matrix, orthonormal_frames, segment_variances, lambda_grid, trait_levels, partition_labels, preceding_fits
+):
+    rows = allele_matrix.shape[0]
+    blocks, width = orthonormal_frames.shape[:2]
+    prot = trait_levels.shape[1]
+    lams = lambda_grid.shape[0]
+    old = preceding_fits[0]
+    old_width = old.shape[1]
+    qw = old_width * nb // n
+    new_width = blocks * lams
+    erows = -(-(nb * new_width + 1) // 16) * 16
+    c_rows, c_cols = blocks * width, FOLDS * prot
+    c_pieces = c_rows // row_piece(c_rows)
+    gp = row_piece(old_width)
+    g_pieces = old_width // gp
+    vmem = pl.BlockSpec(memory_space=pltpu.VMEM)
+    dma = pltpu.SemaphoreType.DMA
+    out = pl.pallas_call(
+        functools.partial(kernel, n, nb, lams),
+        out_shape=(
+            jax.ShapeDtypeStruct((rows, blocks * lams * prot), BF16),
+            jax.ShapeDtypeStruct((old_width, qw), F32),
+            jax.ShapeDtypeStruct((new_width, qw), F32),
+            jax.ShapeDtypeStruct((new_width, nb * new_width), F32),
+            jax.ShapeDtypeStruct((1, qw), F32),
+            jax.ShapeDtypeStruct((new_width, 1), F32),
+        ),
+        in_specs=[vmem, vmem, vmem, pl.BlockSpec(memory_space=pltpu.SMEM), vmem, vmem, vmem],
+        out_specs=(vmem,) * 6,
+        scratch_shapes=[
+            pltpu.VMEM((n, rows, qw), BF16),
+            pltpu.VMEM((old_width, rows), BF16),
+            pltpu.VMEM((blocks, rows, width), BF16),
+            pltpu.VMEM((c_rows, c_cols), F32),
+            pltpu.VMEM((c_rows, c_cols), BF16),
+            pltpu.VMEM((c_rows, c_cols), BF16),
+            pltpu.VMEM((2, c_rows, c_cols), BF16),
+            pltpu.VMEM((n, old_width, qw), BF16),
+            pltpu.VMEM((n, old_width, qw), BF16),
+            pltpu.VMEM((n, old_width, qw), BF16),
+            pltpu.VMEM((gp, qw), F32),
+            pltpu.VMEM((nb, erows, rows), BF16),
+            pltpu.VMEM((erows, rows), BF16),
+            pltpu.VMEM((n, erows, qw + 128), F32),
+            pltpu.VMEM((n, erows, qw + 128), F32),
+            pltpu.VMEM((erows, qw + 128), F32),
+            dma((n, nb)), dma((n,)),
+            dma((2, c_pieces)), dma((2, c_pieces)),
+            dma((n, g_pieces)), dma((n, g_pieces)), dma((n, g_pieces)),
+            dma((nb,)), dma((nb,)), dma((n,)), dma((n,)),
+        ],
+        compiler_params=pltpu.CompilerParams(
+            collective_id=0, has_side_effects=True, vmem_limit_bytes=56 * 1024 * 1024),
+        name="ridge",
+    )(allele_matrix, orthonormal_frames, segment_variances.T, lambda_grid, trait_levels, partition_labels[:, None], old)
+    preds, gram_old, gram_cross, gram_new, fit_old, fit_new = out
+    return (
+        preds.reshape(rows, blocks, lams, prot),
+        gram_old[None],
+        gram_cross[None],
+        gram_new[None],
+        fit_old,
+        fit_new.reshape(1, new_width),
+    )
 
 
 def segment_fitted_trait(
@@ -119,6 +498,24 @@
 
 
 def solution(mesh):
+    n, nb = mesh.shape["smp"], mesh.shape["blk"]
+
+    def program(*arrays):
+        allele_matrix, frames, _, lambda_grid, _, _, preceding_fits = arrays
+        old_width = preceding_fits.shape[2]
+        new_width = frames.shape[0] * lambda_grid.shape[0]
+        fits = (
+            n % 2 == 0
+            and n % nb == 0
+            and (old_width * nb) % (n * 128) == 0
+            and frames.shape[1] % 128 == 0
+            and new_width % 8 == 0
+            and nb * new_width < 128
+        )
+        if fits:
+            return fused(n, nb, *arrays)
+        return per_device(*arrays)
+
     placed = (
         P("smp", ("grp", "blk")),
         P(("grp", "blk"), None, None),
@@ -129,7 +526,7 @@
         P(("grp", "pen"), "smp", "blk"),
     )
     return jax.shard_map(
-        per_device,
+        program,
         mesh=mesh,
         in_specs=placed,
         out_specs=(

time: 205 us -> 87.9 us (0.43)
  waiting for transfers between devices: 153 us -> 0 us
  Pallas kernels: 0 us -> 74.8 us
  between operations: 14 us -> 0.65 us
  blocking collectives: 12.1 us -> 0 us
  matrix products: 11.8 us -> 0 us
  other arithmetic: 11 us -> 1.31 us
  local copies, waits for them, and re-layouts: 3.02 us -> 10.9 us
    pallas_call x0 -> x1, Pallas kernels: none -> 74.8 us  [fused(): pl.pallas_call(functools.partial(kernel, n, nb, lams), out_shape=(jax.Sha...]
    reduce_scatter x1 -> x0, waiting for transfers between devices: 72.1 us -> none  [per_device(): lax.psum_scatter(lax.dot_general(stacked, old_all, contract, preferred_el...]
    psum x1 -> x0, waiting for transfers between devices: 54.1 us -> none  [sum_block(): return lax.psum(local_cross, 'smp')]
    all_gather x1 -> x0, waiting for transfers between devices: 26.7 us -> none  [per_device(): gathered = lax.all_gather(joined, 'blk', axis=1, tiled=True)]
    psum x1 -> x0, blocking collectives: 12.1 us -> none  [per_device(): lax.psum(lax.dot_general(added_columns, right_side, contract, preferred_e...]
    dot_general x14 -> x0, matrix products: 11.8 us -> none  [the longest x1 3.62 us: per_device(): lax.dot_general(stacked, old_all, contract, preferred_element_type=jnp.fl...]
    unnamed x15 -> x12, local copies, waits for them, and re-layouts: 0.62 us -> 7.28 us
    broadcast_in_dim x3 -> x0, other arithmetic: 4.26 us -> none  [the longest x1 2.36 us: per_device(): (gram_old / sample_total)[None]]
  transfers between devices with their start and end apart: 3 -> 0, of which waited for: 3 -> 0; matrix products, arithmetic and copies ran while one was open for 2% -> 0% of each run, Pallas kernels for 0% -> 0%
where the time goes in v1:
time: 87.9 us; the launch traced here: 87.6 us
  Pallas kernels  74.8 us (85%)
  local copies, waits for them, and re-layouts  10.9 us (12%)
  other arithmetic  1.31 us (1%)
    pallas_call x1, Pallas kernels, fused(): pl.pallas_call(functools.partial(kernel, n, nb, lams), out_shape=(jax.Sha...  74.8 us
    unnamed x12, local copies, waits for them, and re-layouts  7.28 us
    pallas_call x1, local copies, waits for them, and re-layouts, fused(): pl.pallas_call(functools.partial(kernel, n, nb, lams), out_shape=(jax.Sha...  2.05 us

profile of v1, /device:TPU:0, one launch (start us, length us, event | category | flops | bytes accessed | tf_op | source)
XLA Modules:
  0.0 87.6 jit_solution(17305270839708384622)
XLA Ops:
  0.6 1.6 %copy.17.trait = bf16[512,64]{1,0:T(8,128)(2,1)} copy(bf16[512,64]{0,1:T(8,128)(2,1)} %param.11) | data formatting | bytes 131072 | tf_op args[4]
  2.2 1.5 %copy.16 = f32[2,512]{0,1:T(8,128)} copy(f32[2,512]{1,0:T(2,128)} %param.9) | data formatting | bytes 8192 | tf_op args[2]
  3.8 1.5 %copy.18.labels = s32[512,1]{1,0:T(8,128)} copy(s32[512,1]{0,1:T(1,128)} %bitcast.14) | data formatting | bytes 4096 | tf_op jit(solution)/shard_map/broadcast_in_dim | solution.py:376
  5.3 74.8 %ridge.1 = (bf16[512,512]{1,0:T(8,128)(2,1)}, f32[768,384]{1,0:T(8,128)}, f32[8,384]{1,0:T(8,128)}, f32[8,16]{1,0:T(8,128)}, f32[1,384]{1,0:T(1,128)}, /*index=5*/f32[8,1]{1,0:T(8,128)}) custom-call(bf16[512,1024]{1,0:T(8,128)(2,1)} %allele.1, bf16[2,512,512]{2,1,0:T(8,128)(2,1)} %frames.1, f32[512,2]{1,0:T(8,128)} %bitcast.9, f32[4]{0:T(128)} %lam.1, ...), custom_call_target="tpu_custom_call" | custom-call | tf_op jit(solution)/shard_map/ridge/pallas_call | solution.py:339
  80.1 2.0 %copy.19 = bf16[512,512]{0,1:T(8,128)(2,1)} copy(bf16[512,512]{1,0:T(8,128)(2,1)} %get-tuple-element.12) | data formatting | bytes 1048576 | tf_op jit(solution)/shard_map/ridge/pallas_call | solution.py:339
  82.1 1.3 %reduce = f32[8]{0:T(128)} reduce(f32[8,1]{1,0:T(8,128)} %get-tuple-element.17, f32[]{:T(128)} %constant.3), dimensions={1}, to_apply=%get-tuple-element.17.reduce_sub_computation | reduce | bytes 68 | tf_op jit(solution)/shard_map/ridge/pallas_call | solution.py:339
  83.4 0.0 copy-start
  83.4 0.0 copy-start.1
  83.4 0.0 copy-start.2
  83.4 2.4 %copy.24 = f32[1,768,384]{2,1,0:T(8,128)} copy(f32[1,768,384]{2,1,0:T(8,128)} %bitcast.8) | data formatting | bytes 2359296
  85.8 0.0 copy-done
  85.8 0.6 copy.25
  86.4 0.0 copy-done.1
  86.4 0.6 copy.26
  87.0 0.0 copy-done.2
  87.0 0.6 copy.27
Async XLA Ops:
  83.4 2.4 %copy-start = (f32[8,384]{1,0:T(8,128)S(1)}, f32[8,384]{1,0:T(8,128)}, u32[]{:S(2)}) copy-start(f32[8,384]{1,0:T(8,128)} %get-tuple-element.14) | copy-start | bytes 36868
  83.4 3.0 %copy-start.1 = (f32[8,16]{1,0:T(8,128)S(1)}, f32[8,16]{1,0:T(8,128)}, u32[]{:S(2)}) copy-start(f32[8,16]{1,0:T(8,128)} %get-tuple-element.15) | copy-start | bytes 1540
  83.4 3.6 %copy-start.2 = (f32[1,384]{1,0:T(1,128)S(1)}, f32[1,384]{1,0:T(1,128)}, u32[]{:S(2)}) copy-start(f32[1,384]{1,0:T(1,128)} %get-tuple-element.34) | copy-start | bytes 4612

commit v2 on v1

--- a/solution.py
+++ b/solution.py
@@ -1,5 +1,4 @@
 import functools
-import math
 
 import jax
 import jax.numpy as jnp
@@ -21,9 +20,9 @@
 def kernel(
     n, nb, groups,
     allele, frames, variances, lam, trait, labels, old,
-    preds_out, gram_out, cross_out, new_out, fit_old_out, fit_new_out,
+    preds_out, gram_out, small_out,
     oldq, old_t, rot, part, c_left, c_right, c_send,
-    g_left, g_right, g_send, g_part, et_all, lhs, m_send, m_recv, m_sum,
+    g_left, g_right, g_send, g_part, et_all, lhs, m_send, m_recv,
     x_send, x_recv, cs_send, cs_recv, gs_send, gl_recv, gr_recv,
     e_send, e_recv, ms_send, ms_recv,
 ):
@@ -31,12 +30,13 @@
     x = lax.axis_index("blk")
     rows, old_width = old.shape
     blocks, width = frames.shape[0], frames.shape[1]
-    prot = trait.shape[1]
+    prot = trait.shape[0]
     lams = groups
     per = n // nb
     qw = old_width // per
-    cp = row_piece(blocks * width)
-    c_pieces = blocks * width // cp
+    c_rows = FOLDS * prot
+    cp = 128
+    c_pieces = blocks * c_rows // cp
     gp = row_piece(old_width)
     g_pieces = old_width // gp
     new_width = blocks * lams
@@ -72,9 +72,8 @@
 
     label = labels[...]
     y = trait[...]
-    y_wide = jnp.concatenate([y] * FOLDS, axis=1)
-    fold_of = lax.broadcasted_iota(jnp.int32, (rows, FOLDS * prot), 1) // prot
-    masked = jnp.where(label == fold_of, y_wide.astype(F32), 0.0).astype(BF16)
+    y_wide = y.astype(F32)
+    masked = jnp.concatenate([jnp.where(label == k, y_wide, 0.0).astype(BF16) for k in range(FOLDS)], axis=0)
 
     def c_copy(p, right):
         piece = pl.ds(p * cp, cp)
@@ -87,9 +86,8 @@
     for b in range(blocks):
         r = jnp.dot(allele[:, b * width:(b + 1) * width], frames[b], preferred_element_type=F32).astype(BF16)
         rot[b] = r
-        part[b * width:(b + 1) * width, :] = lax.dot_general(
-            r, masked, (((0,), (0,)), ((), ())), preferred_element_type=F32)
-        for p in range(b * width // cp, (b + 1) * width // cp):
+        part[b * c_rows:(b + 1) * c_rows, :] = jnp.dot(masked, r, preferred_element_type=F32)
+        for p in range(b * c_rows // cp, (b + 1) * c_rows // cp):
             value = part[p * cp:(p + 1) * cp, :].astype(BF16)
 
             @pl.when(z == 0)
@@ -105,10 +103,11 @@
     for h in range(per):
         oldq[x * per + h] = old[:, h * qw:(h + 1) * qw]
     old_t[...] = old[...].T
-    for q in order:
-        @pl.when(x != q // per)
-        def _():
-            x_wait(q)
+    def wait_for(some, who):
+        for q in some:
+            @pl.when(jnp.logical_and(x != q // per, who))
+            def _():
+                x_wait(q)
 
     def g_copy(q, h, right):
         piece = pl.ds(pl.multiple_of(h * gp, gp), gp)
@@ -162,9 +161,15 @@
     in_left = z < n // 2
     is_end = jnp.logical_or(z == 0, z == n - 1)
 
-    @pl.when(is_end)
-    def _():
-        g_group(jnp.where(in_left, n - 1, 0))
+    is_inner = jnp.logical_not(is_end)
+    wait_for(order[:2], is_end)
+    for i in range(n // 2):
+        if i == 1:
+            wait_for(order[2:], is_end)
+
+        @pl.when(is_end)
+        def _():
+            g_group(jnp.where(in_left, n - 1 - i, i))
 
     def from_side(p, right):
         piece = slice(p * cp, (p + 1) * cp)
@@ -191,6 +196,12 @@
             def _():
                 from_side(p, not first)
 
+    wait_for(order, is_inner)
+
+    @pl.when(is_inner)
+    def _():
+        g_group(jnp.where(in_left, n - 1, 0))
+
     @pl.when(z > 0)
     def _():
         part[...] += c_left[...].astype(F32)
@@ -199,30 +210,28 @@
     def _():
         part[...] += c_right[...].astype(F32)
 
-    lam_lane = lax.broadcasted_iota(jnp.int32, (1, lams * prot), 1) // prot
-    lam_wide = jnp.zeros((1, lams * prot), F32)
-    for r in range(lams):
-        lam_wide = jnp.where(lam_lane == r, lam[r], lam_wide)
     sel_rows = lax.broadcasted_iota(jnp.int32, (erows, lams * prot), 0)
     sel_cols = lax.broadcasted_iota(jnp.int32, (erows, lams * prot), 1)
     e0 = jnp.zeros((erows, rows), F32)
     for b in range(blocks):
-        damp = 1.0 / (variances[:, b:b + 1] + lam_wide)
-        c = part[b * width:(b + 1) * width, :]
-        folds = [c[:, k * prot:(k + 1) * prot] for k in range(FOLDS)]
+        damp = [1.0 / (variances[b:b + 1, :] + lam[r]) for r in range(lams)]
+        folds = [part[b * c_rows + k * prot:b * c_rows + (k + 1) * prot, :] for k in range(FOLDS)]
         total = folds[0]
         for k in range(1, FOLDS):
             total = total + folds[k]
-        acc = jnp.zeros((rows, lams * prot), F32)
+        acc = jnp.zeros((lams * prot, rows), F32)
         for k in range(FOLDS):
-            rest = jnp.concatenate([total - folds[k]] * lams, axis=1)
-            coeff = (rest * damp).astype(BF16)
-            acc = jnp.where(label == k, jnp.dot(rot[b], coeff, preferred_element_type=F32), acc)
+            rest = total - folds[k]
+            coeff = jnp.concatenate([(rest * damp[r]).astype(BF16) for r in range(lams)], axis=0)
+            acc = jnp.where(
+                label == k,
+                lax.dot_general(coeff, rot[b], (((1,), (1,)), ((), ())), preferred_element_type=F32),
+                acc)
         pred = acc.astype(BF16)
-        preds_out[:, b * lams * prot:(b + 1) * lams * prot] = pred
+        preds_out[b * lams * prot:(b + 1) * lams * prot, :] = pred
         wanted = x * new_width + b * lams + sel_cols // prot
         sel = jnp.where(jnp.logical_and(sel_rows == wanted, sel_cols % prot == 0), 1.0, 0.0).astype(BF16)
-        e0 = e0 + lax.dot_general(sel, pred, (((1,), (1,)), ((), ())), preferred_element_type=F32)
+        e0 = e0 + jnp.dot(sel, pred, preferred_element_type=F32)
     et_all[x] = e0.astype(BF16)
 
     def e_copy(d):
@@ -241,7 +250,7 @@
     t_rows = lax.broadcasted_iota(jnp.int32, (erows, prot), 0)
     t_cols = lax.broadcasted_iota(jnp.int32, (erows, prot), 1)
     t_sel = jnp.where(jnp.logical_and(t_rows == nb * new_width, t_cols == 0), 1.0, 0.0).astype(BF16)
-    target = lax.dot_general(t_sel, y, (((1,), (1,)), ((), ())), preferred_element_type=F32)
+    target = jnp.dot(t_sel, y, preferred_element_type=F32)
     lhs[...] = (e0 + target).astype(BF16)
     for q in range(n):
         m_send[q, :, :qw] = jnp.dot(lhs[...], oldq[q], preferred_element_type=F32)
@@ -267,12 +276,8 @@
     for i in range(n // 2):
         early = jnp.where(in_left, n - 1 - i, i)
         late = n - 1 - early
-        if i == 0:
-            @pl.when(jnp.logical_not(is_end))
-            def _():
-                g_group(early)
-        else:
-            @pl.when(early != z)
+        if i > 0:
+            @pl.when(jnp.logical_and(early != z, is_inner))
             def _():
                 g_group(early)
 
@@ -285,14 +290,7 @@
     for d in range(1, n):
         m_copy(d).wait_recv()
         total = total + m_recv[d]
-    m_sum[...] = total / sample_total
-    mine = pl.ds(pl.multiple_of(x * new_width, 8), new_width)
-    cross_out[...] = m_sum[mine, :qw]
-    tail = m_sum[mine, qw:]
-    new_out[...] = tail[:, :nb * new_width]
-    lane = lax.broadcasted_iota(jnp.int32, tail.shape, 1)
-    fit_new_out[...] = jnp.sum(jnp.where(lane == nb * new_width, tail, 0.0), axis=1, keepdims=True)
-    fit_old_out[...] = m_sum[nb * new_width:nb * new_width + 1, :qw]
+    small_out[...] = total / sample_total
 
     for q in range(n):
         @pl.when(x == q // per)
@@ -316,6 +314,25 @@
         def _():
             for h in range(g_pieces):
                 g_copy(q, h, True).wait_send()
+
+
+def finish(nb, new_width, preds, gram, small, preds_out, gram_out, cross_out, new_out, fit_old_out, fit_new_out):
+    preds_out[...] = preds[...]
+    gram_out[0] = gram[...]
+    qw = gram.shape[1]
+
+    @pl.when(pl.program_id(0) == 0)
+    def _():
+        x = lax.axis_index("blk")
+        mine = pl.ds(pl.multiple_of(x * new_width, 8), new_width)
+        cross_out[0] = small[mine, :qw]
+        new_out[0] = small[mine, qw:qw + nb * new_width]
+        fit_old_out[...] = small[nb * new_width:nb * new_width + 1, :qw]
+        row = small[nb * new_width:nb * new_width + 1, qw:]
+        fit = row[:, :new_width]
+        for b in range(1, nb):
+            fit = jnp.where(x == b, row[:, b * new_width:(b + 1) * new_width], fit)
+        fit_new_out[...] = fit
 
 
 def fused(
@@ -330,8 +347,8 @@
     qw = old_width * nb // n
     new_width = blocks * lams
     erows = -(-(nb * new_width + 1) // 16) * 16
-    c_rows, c_cols = blocks * width, FOLDS * prot
-    c_pieces = c_rows // row_piece(c_rows)
+    c_rows, c_cols = blocks * FOLDS * prot, width
+    c_pieces = c_rows // 128
     gp = row_piece(old_width)
     g_pieces = old_width // gp
     vmem = pl.BlockSpec(memory_space=pltpu.VMEM)
@@ -339,15 +356,12 @@
     out = pl.pallas_call(
         functools.partial(kernel, n, nb, lams),
         out_shape=(
-            jax.ShapeDtypeStruct((rows, blocks * lams * prot), BF16),
+            jax.ShapeDtypeStruct((blocks * lams * prot, rows), BF16),
             jax.ShapeDtypeStruct((old_width, qw), F32),
-            jax.ShapeDtypeStruct((new_width, qw), F32),
-            jax.ShapeDtypeStruct((new_width, nb * new_width), F32),
-            jax.ShapeDtypeStruct((1, qw), F32),
-            jax.ShapeDtypeStruct((new_width, 1), F32),
+            jax.ShapeDtypeStruct((erows, qw + 128), F32),
         ),
         in_specs=[vmem, vmem, vmem, pl.BlockSpec(memory_space=pltpu.SMEM), vmem, vmem, vmem],
-        out_specs=(vmem,) * 6,
+        out_specs=(vmem,) * 3,
         scratch_shapes=[
             pltpu.VMEM((n, rows, qw), BF16),
             pltpu.VMEM((old_width, rows), BF16),
@@ -364,7 +378,6 @@
             pltpu.VMEM((erows, rows), BF16),
             pltpu.VMEM((n, erows, qw + 128), F32),
             pltpu.VMEM((n, erows, qw + 128), F32),
-            pltpu.VMEM((erows, qw + 128), F32),
             dma((n, nb)), dma((n,)),
             dma((2, c_pieces)), dma((2, c_pieces)),
             dma((n, g_pieces)), dma((n, g_pieces)), dma((n, g_pieces)),
@@ -373,16 +386,38 @@
         compiler_params=pltpu.CompilerParams(
             collective_id=0, has_side_effects=True, vmem_limit_bytes=56 * 1024 * 1024),
         name="ridge",
-    )(allele_matrix, orthonormal_frames, segment_variances.T, lambda_grid, trait_levels, partition_labels[:, None], old)
-    preds, gram_old, gram_cross, gram_new, fit_old, fit_new = out
-    return (
-        preds.reshape(rows, blocks, lams, prot),
-        gram_old[None],
-        gram_cross[None],
-        gram_new[None],
-        fit_old,
-        fit_new.reshape(1, new_width),
-    )
+    )(allele_matrix, orthonormal_frames, segment_variances, lambda_grid, trait_levels.T, partition_labels[None], old)
+    steps = 4
+    p_rows, g_rows = out[0].shape[0] // steps, old_width // steps
+    whole = lambda *shape: pl.BlockSpec(shape, lambda i: (0,) * len(shape))
+    preds, gram_old, gram_cross, gram_new, fit_old, fit_new = pl.pallas_call(
+        functools.partial(finish, nb, new_width),
+        grid=(steps,),
+        out_shape=(
+            jax.ShapeDtypeStruct(out[0].shape, BF16),
+            jax.ShapeDtypeStruct((1, old_width, qw), F32),
+            jax.ShapeDtypeStruct((1, new_width, qw), F32),
+            jax.ShapeDtypeStruct((1, new_width, nb * new_width), F32),
+            jax.ShapeDtypeStruct((1, qw), F32),
+            jax.ShapeDtypeStruct((1, new_width), F32),
+        ),
+        in_specs=[
+            pl.BlockSpec((p_rows, rows), lambda i: (i, 0)),
+            pl.BlockSpec((g_rows, qw), lambda i: (i, 0)),
+            whole(erows, qw + 128),
+        ],
+        out_specs=(
+            pl.BlockSpec((p_rows, rows), lambda i: (i, 0)),
+            pl.BlockSpec((1, g_rows, qw), lambda i: (0, i, 0)),
+            whole(1, new_width, qw),
+            whole(1, new_width, nb * new_width),
+            whole(1, qw),
+            whole(1, new_width),
+        ),
+        name="finish",
+    )(*out)
+    preds = preds.reshape(blocks, lams, prot, rows).transpose(3, 0, 1, 2)
+    return preds, gram_old, gram_cross, gram_new, fit_old, fit_new
 
 
 def segment_fitted_trait(
@@ -501,7 +536,7 @@
     n, nb = mesh.shape["smp"], mesh.shape["blk"]
 
     def program(*arrays):
-        allele_matrix, frames, _, lambda_grid, _, _, preceding_fits = arrays
+        _, frames, _, lambda_grid, trait_levels, _, preceding_fits = arrays
         old_width = preceding_fits.shape[2]
         new_width = frames.shape[0] * lambda_grid.shape[0]
         fits = (
@@ -510,6 +545,8 @@
             and (old_width * nb) % (n * 128) == 0
             and frames.shape[1] % 128 == 0
             and new_width % 8 == 0
+            and old_width % 64 == 0
+            and FOLDS * trait_levels.shape[1] % 128 == 0
             and nb * new_width < 128
         )
         if fits:

time: 87.9 us -> 67.5 us (0.77)
  local copies, waits for them, and re-layouts: 10.9 us -> 0 us
  Pallas kernels: 74.8 us -> 66.7 us
  other arithmetic: 1.31 us -> 0 us
    pallas_call x1, Pallas kernels: 74.8 us -> 62.8 us  [fused(): pl.pallas_call(functools.partial(kernel, n, nb, lams), out_shape=(jax.Sha...]
    unnamed x12 -> x0, local copies, waits for them, and re-layouts: 7.28 us -> none
    pallas_call x0 -> x1, Pallas kernels: none -> 3.83 us  [fused(): pl.pallas_call(functools.partial(finish, nb, new_width), grid=(steps,), o...]
    pallas_call x1 -> x0, local copies, waits for them, and re-layouts: 2.05 us -> none  [fused(): pl.pallas_call(functools.partial(kernel, n, nb, lams), out_shape=(jax.Sha...]
    broadcast_in_dim x1 -> x0, local copies, waits for them, and re-layouts: 1.53 us -> none  [fused(): partition_labels[:, None]]
    pallas_call x1 -> x0, other arithmetic: 1.31 us -> none  [fused(): pl.pallas_call(functools.partial(kernel, n, nb, lams), out_shape=(jax.Sha...]
where the time goes in v2:
time: 67.5 us; the launch traced here: 67.3 us
  Pallas kernels  66.7 us (99%)
    pallas_call x1, Pallas kernels, fused(): pl.pallas_call(functools.partial(kernel, n, nb, lams), out_shape=(jax.Sha...  62.8 us
    pallas_call x1, Pallas kernels, fused(): pl.pallas_call(functools.partial(finish, nb, new_width), grid=(steps,), o...  3.83 us

profile of v2, /device:TPU:0, one launch (start us, length us, event | category | flops | bytes accessed | tf_op | source)
XLA Modules:
  0.0 67.3 jit_solution(2970574910206898191)
XLA Ops:
  0.6 62.8 %ridge.1 = (bf16[512,512]{1,0:T(8,128)(2,1)}, f32[768,384]{1,0:T(8,128)}, f32[32,512]{1,0:T(8,128)}) custom-call(bf16[512,1024]{1,0:T(8,128)(2,1)} %allele.1, bf16[2,512,512]{2,1,0:T(8,128)(2,1)} %frames.1, f32[2,512]{1,0:T(2,128)} %variances.1, f32[4]{0:T(128)} %lam.1, bf16[64,512]{1,0:T(8,128)(2,1)} %bitcast.7, s32[1,512]{1,0:T(1,128)} %bitcast.8, ...), custom_call_target="tpu_custom_call" | custom-call | tf_op jit(solution)/shard_map/ridge/pallas_call | solution.py:356
  63.5 3.8 %finish.1 = (bf16[512,512]{1,0:T(8,128)(2,1)}, f32[1,768,384]{2,1,0:T(8,128)}, f32[1,8,384]{2,1,0:T(8,128)}, f32[1,8,16]{2,1,0:T(8,128)}, f32[1,384]{1,0:T(1,128)}, /*index=5*/f32[1,8]{1,0:T(1,128)}) custom-call(bf16[512,512]{1,0:T(8,128)(2,1)} %get-tuple-element.15.preds, f32[768,384]{1,0:T(8,128)} %get-tuple-element.16.gram, f32[32,512]{1,0:T(8,128)} %get-tuple-element.17.small), custom_call_target="tpu_custom_call" | custom-call | tf_op jit(solution)/shard_map/finish/pallas_call | solution.py:393

commit v3 on v2

--- a/solution.py
+++ b/solution.py
@@ -19,8 +19,9 @@
 
 def kernel(
     n, nb, groups,
-    allele, frames, variances, lam, trait, labels, old,
+    allele_in, frames_in, variances, lam, trait, labels, old_in,
     preds_out, gram_out, small_out,
+    allele, frames, old, preds, gram, in_sem, out_sem, gram_sem,
     oldq, old_t, rot, part, c_left, c_right, c_send,
     g_left, g_right, g_send, g_part, et_all, lhs, m_send, m_recv,
     x_send, x_recv, cs_send, cs_recv, gs_send, gl_recv, gr_recv,
@@ -46,6 +47,12 @@
     for i in range(n // 2):
         order += [n - 1 - i, i]
 
+    loads = [
+        pltpu.make_async_copy(source, place, in_sem.at[i])
+        for i, (source, place) in enumerate(((allele_in, allele), (frames_in, frames), (old_in, old)))
+    ]
+    for load in loads:
+        load.start()
     barrier = pltpu.get_barrier_semaphore()
     for d in range(1, n):
         pl.semaphore_signal(barrier, inc=1, device_id={"smp": lax.rem(z + d, n)}, device_id_type=MESH)
@@ -56,7 +63,7 @@
     def x_copy(q, d):
         cols = pl.ds(pl.multiple_of((q - x * per) * qw, qw), qw)
         return pltpu.make_async_remote_copy(
-            src_ref=old.at[:, cols], dst_ref=oldq.at[q], send_sem=x_send.at[q, d], recv_sem=x_recv.at[q],
+            src_ref=old_in.at[:, cols], dst_ref=oldq.at[q], send_sem=x_send.at[q, d], recv_sem=x_recv.at[q],
             device_id={"blk": lax.rem(x + d, nb)}, device_id_type=MESH)
 
     def x_wait(q):
@@ -83,6 +90,8 @@
             send_sem=cs_send.at[0 if right else 1, p], recv_sem=cs_recv.at[0 if right else 1, p],
             device_id={"smp": jnp.minimum(z + 1, n - 1) if right else jnp.maximum(z - 1, 0)}, device_id_type=MESH)
 
+    loads[0].wait()
+    loads[1].wait()
     for b in range(blocks):
         r = jnp.dot(allele[:, b * width:(b + 1) * width], frames[b], preferred_element_type=F32).astype(BF16)
         rot[b] = r
@@ -100,6 +109,7 @@
                 c_send[1, p * cp:(p + 1) * cp, :] = value
                 c_copy(p, False).start()
 
+    loads[2].wait()
     for h in range(per):
         oldq[x * per + h] = old[:, h * qw:(h + 1) * qw]
     old_t[...] = old[...].T
@@ -117,6 +127,10 @@
             send_sem=gs_send.at[q, h], recv_sem=(gl_recv if right else gr_recv).at[q, h],
             device_id={"smp": jnp.minimum(z + 1, n - 1) if right else jnp.maximum(z - 1, 0)}, device_id_type=MESH)
 
+    def gram_copy(h):
+        piece = pl.ds(pl.multiple_of(h * gp, gp), gp)
+        return pltpu.make_async_copy(gram.at[piece, :], gram_out.at[piece, :], gram_sem.at[h])
+
     def g_piece(q, h):
         piece = pl.ds(pl.multiple_of(h * gp, gp), gp)
         g_part[...] = jnp.dot(old_t[piece, :], oldq[q], preferred_element_type=F32)
@@ -150,7 +164,8 @@
             def _():
                 g_copy(q, h, False).wait_recv()
                 g_part[...] += g_right[q, piece, :].astype(F32)
-            gram_out[piece, :] = g_part[...] / sample_total
+            gram[piece, :] = g_part[...] / sample_total
+            gram_copy(h).start()
 
     def g_group(q):
         def body(h, carry):
@@ -228,10 +243,12 @@
                 lax.dot_general(coeff, rot[b], (((1,), (1,)), ((), ())), preferred_element_type=F32),
                 acc)
         pred = acc.astype(BF16)
-        preds_out[b * lams * prot:(b + 1) * lams * prot, :] = pred
+        preds[b * lams * prot:(b + 1) * lams * prot, :] = pred
         wanted = x * new_width + b * lams + sel_cols // prot
         sel = jnp.where(jnp.logical_and(sel_rows == wanted, sel_cols % prot == 0), 1.0, 0.0).astype(BF16)
         e0 = e0 + jnp.dot(sel, pred, preferred_element_type=F32)
+    preds_copy = pltpu.make_async_copy(preds, preds_out, out_sem)
+    preds_copy.start()
     et_all[x] = e0.astype(BF16)
 
     def e_copy(d):
@@ -292,6 +309,9 @@
         total = total + m_recv[d]
     small_out[...] = total / sample_total
 
+    preds_copy.wait()
+    for h in range(g_pieces):
+        gram_copy(h).wait()
     for q in range(n):
         @pl.when(x == q // per)
         def _():
@@ -316,23 +336,38 @@
                 g_copy(q, h, True).wait_send()
 
 
-def finish(nb, new_width, preds, gram, small, preds_out, gram_out, cross_out, new_out, fit_old_out, fit_new_out):
-    preds_out[...] = preds[...]
-    gram_out[0] = gram[...]
+def finish(
+    nb, new_width, preds_in, gram_in, small, preds_out, gram_out, cross_out, new_out, fit_old_out, fit_new_out,
+    preds, gram, in_sem, out_sem
+):
+    steps = in_sem.shape[0] // 2
+    moves = []
+    for i in range(steps):
+        for k, (source, place, end) in enumerate(((gram_in, gram, gram_out.at[0]), (preds_in, preds, preds_out))):
+            size = source.shape[0] // steps
+            piece = pl.ds(i * size, size)
+            moves.append((
+                pltpu.make_async_copy(source.at[piece, :], place.at[piece, :], in_sem.at[2 * i + k]),
+                pltpu.make_async_copy(place.at[piece, :], end.at[piece, :], out_sem.at[2 * i + k]),
+            ))
+    for load, _ in moves:
+        load.start()
     qw = gram.shape[1]
-
-    @pl.when(pl.program_id(0) == 0)
-    def _():
-        x = lax.axis_index("blk")
-        mine = pl.ds(pl.multiple_of(x * new_width, 8), new_width)
-        cross_out[0] = small[mine, :qw]
-        new_out[0] = small[mine, qw:qw + nb * new_width]
-        fit_old_out[...] = small[nb * new_width:nb * new_width + 1, :qw]
-        row = small[nb * new_width:nb * new_width + 1, qw:]
-        fit = row[:, :new_width]
-        for b in range(1, nb):
-            fit = jnp.where(x == b, row[:, b * new_width:(b + 1) * new_width], fit)
-        fit_new_out[...] = fit
+    x = lax.axis_index("blk")
+    mine = pl.ds(pl.multiple_of(x * new_width, 8), new_width)
+    cross_out[0] = small[mine, :qw]
+    new_out[0] = small[mine, qw:qw + nb * new_width]
+    fit_old_out[...] = small[nb * new_width:nb * new_width + 1, :qw]
+    row = small[nb * new_width:nb * new_width + 1, qw:]
+    fit = row[:, :new_width]
+    for b in range(1, nb):
+        fit = jnp.where(x == b, row[:, b * new_width:(b + 1) * new_width], fit)
+    fit_new_out[...] = fit
+    for load, store in moves:
+        load.wait()
+        store.start()
+    for _, store in moves:
+        store.wait()
 
 
 def fused(
@@ -352,6 +387,7 @@
     gp = row_piece(old_width)
     g_pieces = old_width // gp
     vmem = pl.BlockSpec(memory_space=pltpu.VMEM)
+    hbm = pl.BlockSpec(memory_space=pl.ANY)
     dma = pltpu.SemaphoreType.DMA
     out = pl.pallas_call(
         functools.partial(kernel, n, nb, lams),
@@ -360,9 +396,15 @@
             jax.ShapeDtypeStruct((old_width, qw), F32),
             jax.ShapeDtypeStruct((erows, qw + 128), F32),
         ),
-        in_specs=[vmem, vmem, vmem, pl.BlockSpec(memory_space=pltpu.SMEM), vmem, vmem, vmem],
-        out_specs=(vmem,) * 3,
+        in_specs=[hbm, hbm, vmem, pl.BlockSpec(memory_space=pltpu.SMEM), vmem, vmem, hbm],
+        out_specs=(hbm, hbm, vmem),
         scratch_shapes=[
+            pltpu.VMEM(allele_matrix.shape, BF16),
+            pltpu.VMEM(orthonormal_frames.shape, BF16),
+            pltpu.VMEM(old.shape, BF16),
+            pltpu.VMEM((blocks * lams * prot, rows), BF16),
+            pltpu.VMEM((old_width, qw), F32),
+            dma((3,)), dma, dma((g_pieces,)),
             pltpu.VMEM((n, rows, qw), BF16),
             pltpu.VMEM((old_width, rows), BF16),
             pltpu.VMEM((blocks, rows, width), BF16),
@@ -388,11 +430,8 @@
         name="ridge",
     )(allele_matrix, orthonormal_frames, segment_variances, lambda_grid, trait_levels.T, partition_labels[None], old)
     steps = 4
-    p_rows, g_rows = out[0].shape[0] // steps, old_width // steps
-    whole = lambda *shape: pl.BlockSpec(shape, lambda i: (0,) * len(shape))
     preds, gram_old, gram_cross, gram_new, fit_old, fit_new = pl.pallas_call(
         functools.partial(finish, nb, new_width),
-        grid=(steps,),
         out_shape=(
             jax.ShapeDtypeStruct(out[0].shape, BF16),
             jax.ShapeDtypeStruct((1, old_width, qw), F32),
@@ -401,19 +440,14 @@
             jax.ShapeDtypeStruct((1, qw), F32),
             jax.ShapeDtypeStruct((1, new_width), F32),
         ),
-        in_specs=[
-            pl.BlockSpec((p_rows, rows), lambda i: (i, 0)),
-            pl.BlockSpec((g_rows, qw), lambda i: (i, 0)),
-            whole(erows, qw + 128),
+        in_specs=[hbm, hbm, vmem],
+        out_specs=(hbm, hbm, vmem, vmem, vmem, vmem),
+        scratch_shapes=[
+            pltpu.VMEM(out[0].shape, BF16),
+            pltpu.VMEM(out[1].shape, F32),
+            dma((2 * steps,)), dma((2 * steps,)),
         ],
-        out_specs=(
-            pl.BlockSpec((p_rows, rows), lambda i: (i, 0)),
-            pl.BlockSpec((1, g_rows, qw), lambda i: (0, i, 0)),
-            whole(1, new_width, qw),
-            whole(1, new_width, nb * new_width),
-            whole(1, qw),
-            whole(1, new_width),
-        ),
+        compiler_params=pltpu.CompilerParams(vmem_limit_bytes=56 * 1024 * 1024),
         name="finish",
     )(*out)
     preds = preds.reshape(blocks, lams, prot, rows).transpose(3, 0, 1, 2)

time: 67.5 us -> 66.2 us (0.981)
  Pallas kernels: 66.7 us -> 65.1 us
    pallas_call x1, Pallas kernels: 62.8 us -> 61.3 us  [fused(): pl.pallas_call(functools.partial(kernel, n, nb, lams), out_shape=(jax.Sha...]
where the time goes in v3:
time: 66.2 us; the launch traced here: 65.7 us
  Pallas kernels  65.1 us (98%)
    pallas_call x1, Pallas kernels, fused(): pl.pallas_call(functools.partial(kernel, n, nb, lams), out_shape=(jax.Sha...  61.3 us
    pallas_call x1, Pallas kernels, fused(): pl.pallas_call(functools.partial(finish, nb, new_width), out_shape=(jax.S...  3.73 us

profile of v3, /device:TPU:0, one launch (start us, length us, event | category | flops | bytes accessed | tf_op | source)
XLA Modules:
  0.0 65.7 jit_solution(14683831559047332115)
XLA Ops:
  0.6 61.3 %ridge.1 = (bf16[512,512]{1,0:T(8,128)(2,1)}, f32[768,384]{1,0:T(8,128)}, f32[32,512]{1,0:T(8,128)}) custom-call(bf16[512,1024]{1,0:T(8,128)(2,1)} %allele_in.1, bf16[2,512,512]{2,1,0:T(8,128)(2,1)} %frames_in.1, f32[2,512]{1,0:T(2,128)} %variances.1, f32[4]{0:T(128)} %lam.1, bf16[64,512]{1,0:T(8,128)(2,1)} %bitcast.7, s32[1,512]{1,0:T(1,128)} %bitcast.8, ...), custom_call_target="tpu_custom_call" | custom-call | tf_op jit(solution)/shard_map/ridge/pallas_call | solution.py:392
  62.0 3.7 %finish.1 = (bf16[512,512]{1,0:T(8,128)(2,1)}, f32[1,768,384]{2,1,0:T(8,128)}, f32[1,8,384]{2,1,0:T(8,128)}, f32[1,8,16]{2,1,0:T(8,128)}, f32[1,384]{1,0:T(1,128)}, /*index=5*/f32[1,8]{1,0:T(1,128)}) custom-call(bf16[512,512]{1,0:T(8,128)(2,1)} %get-tuple-element.15.preds_in, f32[768,384]{1,0:T(8,128)} %get-tuple-element.16.gram_in, ...), custom_call_target="tpu_custom_call" | custom-call | tf_op jit(solution)/shard_map/finish/pallas_call | solution.py:433

commit v4 on v3

--- a/solution.py
+++ b/solution.py
@@ -19,9 +19,9 @@
 
 def kernel(
     n, nb, groups,
-    allele_in, frames_in, variances, lam, trait, labels, old_in,
+    allele, frames, variances, lam, trait, labels, old,
     preds_out, gram_out, small_out,
-    allele, frames, old, preds, gram, in_sem, out_sem, gram_sem,
+    preds, gram, out_sem, gram_sem,
     oldq, old_t, rot, part, c_left, c_right, c_send,
     g_left, g_right, g_send, g_part, et_all, lhs, m_send, m_recv,
     x_send, x_recv, cs_send, cs_recv, gs_send, gl_recv, gr_recv,
@@ -47,12 +47,6 @@
     for i in range(n // 2):
         order += [n - 1 - i, i]
 
-    loads = [
-        pltpu.make_async_copy(source, place, in_sem.at[i])
-        for i, (source, place) in enumerate(((allele_in, allele), (frames_in, frames), (old_in, old)))
-    ]
-    for load in loads:
-        load.start()
     barrier = pltpu.get_barrier_semaphore()
     for d in range(1, n):
         pl.semaphore_signal(barrier, inc=1, device_id={"smp": lax.rem(z + d, n)}, device_id_type=MESH)
@@ -63,7 +57,7 @@
     def x_copy(q, d):
         cols = pl.ds(pl.multiple_of((q - x * per) * qw, qw), qw)
         return pltpu.make_async_remote_copy(
-            src_ref=old_in.at[:, cols], dst_ref=oldq.at[q], send_sem=x_send.at[q, d], recv_sem=x_recv.at[q],
+            src_ref=old.at[:, cols], dst_ref=oldq.at[q], send_sem=x_send.at[q, d], recv_sem=x_recv.at[q],
             device_id={"blk": lax.rem(x + d, nb)}, device_id_type=MESH)
 
     def x_wait(q):
@@ -90,8 +84,6 @@
             send_sem=cs_send.at[0 if right else 1, p], recv_sem=cs_recv.at[0 if right else 1, p],
             device_id={"smp": jnp.minimum(z + 1, n - 1) if right else jnp.maximum(z - 1, 0)}, device_id_type=MESH)
 
-    loads[0].wait()
-    loads[1].wait()
     for b in range(blocks):
         r = jnp.dot(allele[:, b * width:(b + 1) * width], frames[b], preferred_element_type=F32).astype(BF16)
         rot[b] = r
@@ -109,7 +101,6 @@
                 c_send[1, p * cp:(p + 1) * cp, :] = value
                 c_copy(p, False).start()
 
-    loads[2].wait()
     for h in range(per):
         oldq[x * per + h] = old[:, h * qw:(h + 1) * qw]
     old_t[...] = old[...].T
@@ -229,7 +220,7 @@
     sel_cols = lax.broadcasted_iota(jnp.int32, (erows, lams * prot), 1)
     e0 = jnp.zeros((erows, rows), F32)
     for b in range(blocks):
-        damp = [1.0 / (variances[b:b + 1, :] + lam[r]) for r in range(lams)]
+        damp = [1.0 / (variances[b:b + 1, :] + lam[0:1, r:r + 1]) for r in range(lams)]
         folds = [part[b * c_rows + k * prot:b * c_rows + (k + 1) * prot, :] for k in range(FOLDS)]
         total = folds[0]
         for k in range(1, FOLDS):
@@ -338,21 +329,15 @@
 
 def finish(
     nb, new_width, preds_in, gram_in, small, preds_out, gram_out, cross_out, new_out, fit_old_out, fit_new_out,
-    preds, gram, in_sem, out_sem
+    sem
 ):
-    steps = in_sem.shape[0] // 2
-    moves = []
-    for i in range(steps):
-        for k, (source, place, end) in enumerate(((gram_in, gram, gram_out.at[0]), (preds_in, preds, preds_out))):
-            size = source.shape[0] // steps
-            piece = pl.ds(i * size, size)
-            moves.append((
-                pltpu.make_async_copy(source.at[piece, :], place.at[piece, :], in_sem.at[2 * i + k]),
-                pltpu.make_async_copy(place.at[piece, :], end.at[piece, :], out_sem.at[2 * i + k]),
-            ))
-    for load, _ in moves:
-        load.start()
-    qw = gram.shape[1]
+    copies = [
+        pltpu.make_async_copy(gram_in, gram_out.at[0], sem.at[0]),
+        pltpu.make_async_copy(preds_in, preds_out, sem.at[1]),
+    ]
+    for copy in copies:
+        copy.start()
+    qw = gram_in.shape[1]
     x = lax.axis_index("blk")
     mine = pl.ds(pl.multiple_of(x * new_width, 8), new_width)
     cross_out[0] = small[mine, :qw]
@@ -363,11 +348,8 @@
     for b in range(1, nb):
         fit = jnp.where(x == b, row[:, b * new_width:(b + 1) * new_width], fit)
     fit_new_out[...] = fit
-    for load, store in moves:
-        load.wait()
-        store.start()
-    for _, store in moves:
-        store.wait()
+    for copy in copies:
+        copy.wait()
 
 
 def fused(
@@ -387,7 +369,7 @@
     gp = row_piece(old_width)
     g_pieces = old_width // gp
     vmem = pl.BlockSpec(memory_space=pltpu.VMEM)
-    hbm = pl.BlockSpec(memory_space=pl.ANY)
+    anywhere = pl.BlockSpec(memory_space=pl.ANY)
     dma = pltpu.SemaphoreType.DMA
     out = pl.pallas_call(
         functools.partial(kernel, n, nb, lams),
@@ -396,15 +378,12 @@
             jax.ShapeDtypeStruct((old_width, qw), F32),
             jax.ShapeDtypeStruct((erows, qw + 128), F32),
         ),
-        in_specs=[hbm, hbm, vmem, pl.BlockSpec(memory_space=pltpu.SMEM), vmem, vmem, hbm],
-        out_specs=(hbm, hbm, vmem),
+        in_specs=[vmem] * 7,
+        out_specs=(anywhere, anywhere, vmem),
         scratch_shapes=[
-            pltpu.VMEM(allele_matrix.shape, BF16),
-            pltpu.VMEM(orthonormal_frames.shape, BF16),
-            pltpu.VMEM(old.shape, BF16),
             pltpu.VMEM((blocks * lams * prot, rows), BF16),
             pltpu.VMEM((old_width, qw), F32),
-            dma((3,)), dma, dma((g_pieces,)),
+            dma, dma((g_pieces,)),
             pltpu.VMEM((n, rows, qw), BF16),
             pltpu.VMEM((old_width, rows), BF16),
             pltpu.VMEM((blocks, rows, width), BF16),
@@ -426,10 +405,9 @@
             dma((nb,)), dma((nb,)), dma((n,)), dma((n,)),
         ],
         compiler_params=pltpu.CompilerParams(
-            collective_id=0, has_side_effects=True, vmem_limit_bytes=56 * 1024 * 1024),
+            collective_id=0, has_side_effects=True, vmem_limit_bytes=28 * 1024 * 1024),
         name="ridge",
-    )(allele_matrix, orthonormal_frames, segment_variances, lambda_grid, trait_levels.T, partition_labels[None], old)
-    steps = 4
+    )(allele_matrix, orthonormal_frames, segment_variances, lambda_grid[None], trait_levels.T, partition_labels[None], old)
     preds, gram_old, gram_cross, gram_new, fit_old, fit_new = pl.pallas_call(
         functools.partial(finish, nb, new_width),
         out_shape=(
@@ -440,14 +418,10 @@
             jax.ShapeDtypeStruct((1, qw), F32),
             jax.ShapeDtypeStruct((1, new_width), F32),
         ),
-        in_specs=[hbm, hbm, vmem],
-        out_specs=(hbm, hbm, vmem, vmem, vmem, vmem),
-        scratch_shapes=[
-            pltpu.VMEM(out[0].shape, BF16),
-            pltpu.VMEM(out[1].shape, F32),
-            dma((2 * steps,)), dma((2 * steps,)),
-        ],
-        compiler_params=pltpu.CompilerParams(vmem_limit_bytes=56 * 1024 * 1024),
+        in_specs=[anywhere, anywhere, vmem],
+        out_specs=(anywhere, anywhere, vmem, vmem, vmem, vmem),
+        scratch_shapes=[dma((2,))],
+        compiler_params=pltpu.CompilerParams(vmem_limit_bytes=4 * 1024 * 1024),
         name="finish",
     )(*out)
     preds = preds.reshape(blocks, lams, prot, rows).transpose(3, 0, 1, 2)

time: 66.2 us -> 69 us (1.042)
  local copies, waits for them, and re-layouts: 0 us -> 6.44 us
  Pallas kernels: 65.1 us -> 61.6 us
    unnamed x0 -> x14, local copies, waits for them, and re-layouts: none -> 6.44 us
    pallas_call x1, Pallas kernels: 3.73 us -> 1.82 us  [fused(): pl.pallas_call(functools.partial(finish, nb, new_width), out_shape=(jax.S...]
    pallas_call x1, Pallas kernels: 61.3 us -> 59.8 us  [fused(): pl.pallas_call(functools.partial(kernel, n, nb, lams), out_shape=(jax.Sha...]
where the time goes in v4:
time: 69 us; the launch traced here: 68.7 us
  Pallas kernels  61.6 us (89%)
  local copies, waits for them, and re-layouts  6.44 us (9%)
    pallas_call x1, Pallas kernels, fused(): pl.pallas_call(functools.partial(kernel, n, nb, lams), out_shape=(jax.Sha...  59.8 us
    unnamed x14, local copies, waits for them, and re-layouts  6.44 us
    pallas_call x1, Pallas kernels, fused(): pl.pallas_call(functools.partial(finish, nb, new_width), out_shape=(jax.S...  1.82 us

profile of v4, /device:TPU:0, one launch (start us, length us, event | category | flops | bytes accessed | tf_op | source)
XLA Modules:
  0.0 68.7 jit_solution(13613459506212221331)
XLA Ops:
  0.6 0.0 copy-start
  0.6 1.2 %copy-done = bf16[512,1024]{1,0:T(8,128)(2,1)S(1)} copy-done((bf16[512,1024]{1,0:T(8,128)(2,1)S(1)}, bf16[512,1024]{1,0:T(8,128)(2,1)}, u32[]{:S(2)}) %copy-start) | copy-done | bytes 1048600
  1.9 0.0 copy-start.1
  1.9 1.2 %copy-done.1 = bf16[2,512,512]{2,1,0:T(8,128)(2,1)S(1)} copy-done((bf16[2,512,512]{2,1,0:T(8,128)(2,1)S(1)}, bf16[2,512,512]{2,1,0:T(8,128)(2,1)}, u32[]{:S(2)}) %copy-start.1) | copy-done | bytes 1048600
  3.1 0.0 copy-start.2
  3.1 1.1 %copy-done.2 = bf16[1,512,768]{2,1,0:T(8,128)(2,1)S(1)} copy-done((bf16[1,512,768]{2,1,0:T(8,128)(2,1)S(1)}, bf16[1,512,768]{2,1,0:T(8,128)(2,1)}, u32[]{:S(2)}) %copy-start.2) | copy-done | bytes 786456
  4.2 0.0 copy-start.3
  4.2 0.8 %copy-done.3 = bf16[512,64]{0,1:T(8,128)(2,1)S(1)} copy-done((bf16[512,64]{0,1:T(8,128)(2,1)S(1)}, bf16[512,64]{0,1:T(8,128)(2,1)}, u32[]{:S(2)}) %copy-start.3) | copy-done | bytes 65560
  5.1 0.0 copy-start.4
  5.1 0.7 copy-done.4
  5.7 0.0 copy-start.5
  5.7 0.7 copy-done.5
  6.4 0.0 copy-start.6
  6.4 0.7 copy-done.6
  7.1 59.8 %ridge.1 = (bf16[512,512]{1,0:T(8,128)(2,1)S(1)}, f32[768,384]{1,0:T(8,128)S(1)}, f32[32,512]{1,0:T(8,128)S(1)}) custom-call(bf16[512,1024]{1,0:T(8,128)(2,1)S(1)} %copy-done, bf16[2,512,512]{2,1,0:T(8,128)(2,1)S(1)} %copy-done.1, f32[2,512]{1,0:T(2,128)S(1)} %copy-done.4, f32[1,4]{1,0:T(1,128)S(1)} %bitcast.10, bf16[64,512]{1,0:T(8,128)(2,1)S(1)} %bitcast.8, ...), custom_call_target="tpu_custom_call" | custom-call | tf_op jit(solution)/shard_map/ridge/pallas_call | solution.py:374
  66.9 1.8 %finish.1 = (bf16[512,512]{1,0:T(8,128)(2,1)}, f32[1,768,384]{2,1,0:T(8,128)}, f32[1,8,384]{2,1,0:T(8,128)}, f32[1,8,16]{2,1,0:T(8,128)}, f32[1,384]{1,0:T(1,128)}, /*index=5*/f32[1,8]{1,0:T(1,128)}) custom-call(bf16[512,512]{1,0:T(8,128)(2,1)S(1)} %get-tuple-element.15.preds_in, f32[768,384]{1,0:T(8,128)S(1)} %get-tuple-element.16.gram_in, ...), custom_call_target="tpu_custom_call" | custom-call | tf_op jit(solution)/shard_map/finish/pallas_call | solution.py:411
Async XLA Ops:
  0.6 1.2 %copy-start = (bf16[512,1024]{1,0:T(8,128)(2,1)S(1)}, bf16[512,1024]{1,0:T(8,128)(2,1)}, u32[]{:S(2)}) copy-start(bf16[512,1024]{1,0:T(8,128)(2,1)} %allele.1) | copy-start | bytes 3145732
  1.9 1.2 %copy-start.1 = (bf16[2,512,512]{2,1,0:T(8,128)(2,1)S(1)}, bf16[2,512,512]{2,1,0:T(8,128)(2,1)}, u32[]{:S(2)}) copy-start(bf16[2,512,512]{2,1,0:T(8,128)(2,1)} %frames.1) | copy-start | bytes 3145732
  3.1 1.1 %copy-start.2 = (bf16[1,512,768]{2,1,0:T(8,128)(2,1)S(1)}, bf16[1,512,768]{2,1,0:T(8,128)(2,1)}, u32[]{:S(2)}) copy-start(bf16[1,512,768]{2,1,0:T(8,128)(2,1)} %param.13) | copy-start | bytes 2359300
  4.2 0.8 %copy-start.3 = (bf16[512,64]{0,1:T(8,128)(2,1)S(1)}, bf16[512,64]{0,1:T(8,128)(2,1)}, u32[]{:S(2)}) copy-start(bf16[512,64]{0,1:T(8,128)(2,1)} %param.11) | copy-start | bytes 196612
  5.1 0.7 %copy-start.4 = (f32[2,512]{1,0:T(2,128)S(1)}, f32[2,512]{1,0:T(2,128)}, u32[]{:S(2)}) copy-start(f32[2,512]{1,0:T(2,128)} %variances.1) | copy-start | bytes 12292
  5.7 0.7 copy-start.5
  6.4 0.7 copy-start.6

commit v5 on v4

--- a/solution.py
+++ b/solution.py
@@ -19,9 +19,9 @@
 
 def kernel(
     n, nb, groups,
-    allele, frames, variances, lam, trait, labels, old,
+    allele_in, frames_in, variances_in, lam_in, trait_in, labels_in, old_in,
     preds_out, gram_out, small_out,
-    preds, gram, out_sem, gram_sem,
+    allele, frames, variances, lam, trait, labels, old, preds, gram, in_sem, out_sem, gram_sem,
     oldq, old_t, rot, part, c_left, c_right, c_send,
     g_left, g_right, g_send, g_part, et_all, lhs, m_send, m_recv,
     x_send, x_recv, cs_send, cs_recv, gs_send, gl_recv, gr_recv,
@@ -47,6 +47,14 @@
     for i in range(n // 2):
         order += [n - 1 - i, i]
 
+    loads = [
+        pltpu.make_async_copy(source, place, in_sem.at[i])
+        for i, (source, place) in enumerate((
+            (allele_in, allele), (frames_in, frames), (trait_in, trait), (labels_in, labels),
+            (old_in, old), (variances_in, variances), (lam_in, lam)))
+    ]
+    for load in loads:
+        load.start()
     barrier = pltpu.get_barrier_semaphore()
     for d in range(1, n):
         pl.semaphore_signal(barrier, inc=1, device_id={"smp": lax.rem(z + d, n)}, device_id_type=MESH)
@@ -57,7 +65,7 @@
     def x_copy(q, d):
         cols = pl.ds(pl.multiple_of((q - x * per) * qw, qw), qw)
         return pltpu.make_async_remote_copy(
-            src_ref=old.at[:, cols], dst_ref=oldq.at[q], send_sem=x_send.at[q, d], recv_sem=x_recv.at[q],
+            src_ref=old_in.at[:, cols], dst_ref=oldq.at[q], send_sem=x_send.at[q, d], recv_sem=x_recv.at[q],
             device_id={"blk": lax.rem(x + d, nb)}, device_id_type=MESH)
 
     def x_wait(q):
@@ -71,6 +79,8 @@
             for d in range(1, nb):
                 x_copy(q, d).start()
 
+    for load in loads[:4]:
+        load.wait()
     label = labels[...]
     y = trait[...]
     y_wide = y.astype(F32)
@@ -101,6 +111,8 @@
                 c_send[1, p * cp:(p + 1) * cp, :] = value
                 c_copy(p, False).start()
 
+    for load in loads[4:]:
+        load.wait()
     for h in range(per):
         oldq[x * per + h] = old[:, h * qw:(h + 1) * qw]
     old_t[...] = old[...].T
@@ -378,12 +390,19 @@
             jax.ShapeDtypeStruct((old_width, qw), F32),
             jax.ShapeDtypeStruct((erows, qw + 128), F32),
         ),
-        in_specs=[vmem] * 7,
+        in_specs=[pl.BlockSpec(memory_space=pltpu.HBM)] * 7,
         out_specs=(anywhere, anywhere, vmem),
         scratch_shapes=[
+            pltpu.VMEM(allele_matrix.shape, BF16),
+            pltpu.VMEM(orthonormal_frames.shape, BF16),
+            pltpu.VMEM(segment_variances.shape, F32),
+            pltpu.VMEM((1, lams), F32),
+            pltpu.VMEM((prot, rows), BF16),
+            pltpu.VMEM((1, rows), jnp.int32),
+            pltpu.VMEM(old.shape, BF16),
             pltpu.VMEM((blocks * lams * prot, rows), BF16),
             pltpu.VMEM((old_width, qw), F32),
-            dma, dma((g_pieces,)),
+            dma((7,)), dma, dma((g_pieces,)),
             pltpu.VMEM((n, rows, qw), BF16),
             pltpu.VMEM((old_width, rows), BF16),
             pltpu.VMEM((blocks, rows, width), BF16),
@@ -407,7 +426,12 @@
         compiler_params=pltpu.CompilerParams(
             collective_id=0, has_side_effects=True, vmem_limit_bytes=28 * 1024 * 1024),
         name="ridge",
-    )(allele_matrix, orthonormal_frames, segment_variances, lambda_grid[None], trait_levels.T, partition_labels[None], old)
+    )(*[
+        pltpu.with_memory_space_constraint(array, pltpu.HBM)
+        for array in (
+            allele_matrix, orthonormal_frames, segment_variances, lambda_grid[None], trait_levels.T,
+            partition_labels[None], old)
+    ])
     preds, gram_old, gram_cross, gram_new, fit_old, fit_new = pl.pallas_call(
         functools.partial(finish, nb, new_width),
         out_shape=(

time: 69 us -> 62.5 us (0.906)
  local copies, waits for them, and re-layouts: 6.44 us -> 0 us
    unnamed x14 -> x0, local copies, waits for them, and re-layouts: 6.44 us -> none
where the time goes in v5:
time: 62.5 us; the launch traced here: 62.3 us
  Pallas kernels  61.7 us (99%)
  between operations  0.64 us (1%)
    pallas_call x1, Pallas kernels, fused(): pl.pallas_call(functools.partial(kernel, n, nb, lams), out_shape=(jax.Sha...  59.9 us
    pallas_call x1, Pallas kernels, fused(): pl.pallas_call(functools.partial(finish, nb, new_width), out_shape=(jax.S...  1.82 us

profile of v5, /device:TPU:0, one launch (start us, length us, event | category | flops | bytes accessed | tf_op | source)
XLA Modules:
  0.0 62.3 jit_solution(14904944237969415224)
XLA Ops:
  0.6 59.9 %ridge.1 = (bf16[512,512]{1,0:T(8,128)(2,1)S(1)}, f32[768,384]{1,0:T(8,128)S(1)}, f32[32,512]{1,0:T(8,128)S(1)}) custom-call(bf16[512,1024]{1,0:T(8,128)(2,1)} %allele_in.1, bf16[2,512,512]{2,1,0:T(8,128)(2,1)} %frames_in.1, f32[2,512]{1,0:T(2,128)} %variances_in.1, f32[1,4]{1,0:T(1,128)} %bitcast.10, bf16[64,512]{1,0:T(8,128)(2,1)} %bitcast.8, ...), custom_call_target="tpu_custom_call" | custom-call | tf_op jit(solution)/shard_map/ridge/pallas_call | solution.py:386
  60.5 1.8 %finish.1 = (bf16[512,512]{1,0:T(8,128)(2,1)}, f32[1,768,384]{2,1,0:T(8,128)}, f32[1,8,384]{2,1,0:T(8,128)}, f32[1,8,16]{2,1,0:T(8,128)}, f32[1,384]{1,0:T(1,128)}, /*index=5*/f32[1,8]{1,0:T(1,128)}) custom-call(bf16[512,512]{1,0:T(8,128)(2,1)S(1)} %get-tuple-element.15.preds_in, f32[768,384]{1,0:T(8,128)S(1)} %get-tuple-element.16.gram_in, ...), custom_call_target="tpu_custom_call" | custom-call | tf_op jit(solution)/shard_map/finish/pallas_call | solution.py:435
